TPU v7x, 32 devices: a whole 2x2x4 slice. The times are simulated.
32 devices in a mesh: dp: 8 (over y, x, core), tensor: 4 (over z).
Axes of the slice: x: 2, y: 2, z: 4, core: 2. Of those that a mesh axis runs over, the one named last changes fastest.
Arguments:
- tokens: bfloat16 [8192, 2048], P(('dp', 'tensor')), may hold values from -6 to 6
- lengths: int32 [8], P('dp'), may hold values from 256 to 1024, as said below
- ln1_gain: bfloat16 [2048], P('dp'), may hold values from 0.5 to 1.5
- ln1_bias: bfloat16 [2048], P('dp'), may hold values from -4 to 4
- qkv_weight: bfloat16 [2048, 3, 2048], P('dp', None, 'tensor'), may hold values from -0.125 to 0.125
- qv_bias: bfloat16 [2, 16, 128], P(None, 'tensor', 'dp'), may hold values from -4 to 4
- out_weight: bfloat16 [2048, 2048], P('tensor', 'dp'), may hold values from -0.75 to 0.75
- out_bias: bfloat16 [2048], P('dp'), may hold values from -4 to 4
- ln2_gain: bfloat16 [2048], P('dp'), may hold values from 0.5 to 1.5
- ln2_bias: bfloat16 [2048], P('dp'), may hold values from -4 to 4
- up_weight: bfloat16 [2048, 8192], P('dp', 'tensor'), may hold values from -0.125 to 0.125
- up_bias: bfloat16 [512, 16], P('tensor', 'dp'), may hold values from -4 to 4
- down_weight: bfloat16 [8192, 2048], P('tensor', 'dp'), may hold values from -0.0625 to 0.0625
- down_bias: bfloat16 [2048], P('dp'), may hold values from -4 to 4
- cotangent: bfloat16 [8192, 2048], P(('dp', 'tensor')), may hold values from -6 to 6
Outputs:
- output: bfloat16 [8192, 2048], P(('dp', 'tensor'))
- tokens_grad: float32 [8192, 2048], P(('dp', 'tensor'))
- ln1_gain_grad: float32 [2048], P('dp')
- ln1_bias_grad: float32 [2048], P('dp')
- qkv_weight_grad: float32 [2048, 3, 2048], P('dp', None, 'tensor')
- qv_bias_grad: float32 [2, 16, 128], P(None, 'tensor', 'dp')
- out_weight_grad: float32 [2048, 2048], P('tensor', 'dp')
- out_bias_grad: float32 [2048], P('dp')
- ln2_gain_grad: float32 [2048], P('dp')
- ln2_bias_grad: float32 [2048], P('dp')
- up_weight_grad: float32 [2048, 8192], P('dp', 'tensor')
- up_bias_grad: float32 [512, 16], P('tensor', 'dp')
- down_weight_grad: float32 [8192, 2048], P('tensor', 'dp')
- down_bias_grad: float32 [2048], P('dp')
- stream_rms: float32 [5], replicated
Inputs may be any that keep to these rules, and one draw needn't show every extreme that they name: `lengths`: each sequence's true token count.
All inputs are finite; a program needn't handle non-finite values.
Results may differ from a plain program's by a relative error of at most 0.02.
Values may be sent and summed in bfloat16 or wider, within the bound.
A program may use at most 256 MiB of HBM per device.

v0:
```python
import jax
import jax.numpy as jnp
from jax import lax
from jax.sharding import PartitionSpec as P

D = 2048
HD = 128
LEN = 1024
EPS = 1e-05


def layer_norm(values, norm_gain, norm_shift):
    center = values - jnp.mean(values, axis=-1, keepdims=True)
    spread = lax.rsqrt(jnp.mean(center * center, axis=-1, keepdims=True) + EPS)
    normed = center * spread
    return (normed * norm_gain + norm_shift, normed, spread)


def norm_backward(upstream, normed, spread, norm_gain):
    scaled = upstream * norm_gain
    mean_part = jnp.mean(scaled, axis=-1, keepdims=True)
    across = jnp.mean(scaled * normed, axis=-1, keepdims=True)
    return spread * (scaled - mean_part - normed * across)


def gelu_tanh(values):
    return jax.nn.gelu(values, approximate=True)


def contract_rows(left, right):
    return lax.dot_general(
        left, right, (((0,), (0,)), ((), ())), preferred_element_type=jnp.float32
    )


def contract_cols(left, right):
    return lax.dot_general(
        left, right, (((1,), (1,)), ((), ())), preferred_element_type=jnp.float32
    )


def allowed_keys(first_row, block_size, positions, length):
    query_pos = first_row + jnp.arange(block_size, dtype=jnp.int32)
    return (positions[None, :] <= query_pos[:, None]) & (positions[None, :] < length)


def attend_forward(queries, key_rows, value_rows, length):
    block_size = min(512, LEN)
    positions = jnp.arange(LEN, dtype=jnp.int32)
    score_scale = HD ** (-0.5)

    def one_block(block_index):
        first_row = block_index * block_size
        query_block = lax.dynamic_slice_in_dim(queries, first_row, block_size, 0)
        scores = (
            jnp.einsum("qhd,khd->hqk", query_block, key_rows, preferred_element_type=jnp.float32)
            * score_scale
        )
        allowed = allowed_keys(first_row, block_size, positions, length)
        scores = jnp.where(allowed[None], scores, -1e30)
        row_max = jnp.max(scores, axis=-1, keepdims=True)
        powers = jnp.exp(scores - row_max)
        totals = jnp.sum(powers, axis=-1, keepdims=True)
        shares = (powers / totals).astype(jnp.bfloat16)
        mixed = jnp.einsum("hqk,khd->qhd", shares, value_rows, preferred_element_type=jnp.float32)
        return (mixed.astype(jnp.bfloat16), (row_max + jnp.log(totals))[..., 0])

    mixed, log_totals = lax.map(one_block, jnp.arange(LEN // block_size, dtype=jnp.int32))
    return (mixed.reshape(LEN, queries.shape[1], HD), log_totals)


def attend_backward(queries, key_rows, value_rows, grad_out, log_totals, length):
    block_size = min(512, LEN)
    positions = jnp.arange(LEN, dtype=jnp.int32)
    score_scale = HD ** (-0.5)

    def one_block(carry, block_index):
        key_grad, value_grad = carry
        first_row = block_index * block_size
        query_block = lax.dynamic_slice_in_dim(queries, first_row, block_size, 0)
        grad_block = lax.dynamic_slice_in_dim(grad_out, first_row, block_size, 0)
        scores = (
            jnp.einsum("qhd,khd->hqk", query_block, key_rows, preferred_element_type=jnp.float32)
            * score_scale
        )
        allowed = allowed_keys(first_row, block_size, positions, length)
        shares = jnp.where(allowed[None], jnp.exp(scores - log_totals[block_index][..., None]), 0.0)
        value_grad = value_grad + jnp.einsum(
            "hqk,qhd->khd",
            shares.astype(jnp.bfloat16),
            grad_block,
            preferred_element_type=jnp.float32,
        )
        share_grad = jnp.einsum(
            "qhd,khd->hqk", grad_block, value_rows, preferred_element_type=jnp.float32
        )
        centre = jnp.sum(shares * share_grad, axis=-1, keepdims=True)
        score_grad = (shares * (share_grad - centre)).astype(jnp.bfloat16)
        query_grad = (
            jnp.einsum("hqk,khd->qhd", score_grad, key_rows, preferred_element_type=jnp.float32)
            * score_scale
        )
        key_grad = (
            key_grad
            + jnp.einsum(
                "hqk,qhd->khd", score_grad, query_block, preferred_element_type=jnp.float32
            )
            * score_scale
        )
        return ((key_grad, value_grad), query_grad.astype(jnp.bfloat16))

    zeros_kv = jnp.zeros((LEN, queries.shape[1], HD), jnp.float32)
    (key_grad, value_grad), query_grads = lax.scan(
        one_block, (zeros_kv, zeros_kv), jnp.arange(LEN // block_size, dtype=jnp.int32)
    )
    return (
        query_grads.reshape(LEN, queries.shape[1], HD),
        key_grad.astype(jnp.bfloat16),
        value_grad.astype(jnp.bfloat16),
    )


def shards(
    tokens,
    lengths,
    ln1_gain,
    ln1_bias,
    qkv_weight,
    qv_bias,
    out_weight,
    out_bias,
    ln2_gain,
    ln2_bias,
    up_weight,
    up_bias,
    down_weight,
    down_bias,
    cotangent,
):
    (
        gain_one,
        shift_one,
        qkv_full,
        qv_full,
        out_full,
        out_shift,
        gain_two,
        shift_two,
        up_full,
        up_shift,
        down_full,
        down_shift,
    ) = (
        lax.all_gather(ln1_gain, "dp", axis=0, tiled=True),
        lax.all_gather(ln1_bias, "dp", axis=0, tiled=True),
        lax.all_gather(qkv_weight, "dp", axis=0, tiled=True),
        lax.all_gather(qv_bias, "dp", axis=2, tiled=True),
        lax.all_gather(out_weight, "dp", axis=1, tiled=True),
        lax.all_gather(out_bias, "dp", axis=0, tiled=True),
        lax.all_gather(ln2_gain, "dp", axis=0, tiled=True),
        lax.all_gather(ln2_bias, "dp", axis=0, tiled=True),
        lax.all_gather(up_weight, "dp", axis=0, tiled=True),
        lax.all_gather(up_bias, "dp", axis=1, tiled=True),
        lax.all_gather(down_weight, "dp", axis=1, tiled=True),
        lax.all_gather(down_bias, "dp", axis=0, tiled=True),
    )
    gain_one = gain_one.astype(jnp.float32)
    shift_one = shift_one.astype(jnp.float32)
    gain_two = gain_two.astype(jnp.float32)
    shift_two = shift_two.astype(jnp.float32)
    out_shift = out_shift.astype(jnp.float32)
    down_shift = down_shift.astype(jnp.float32)
    own_rows = tokens.shape[0]
    group_rows = own_rows * lax.axis_size("tensor")
    seq_count = lengths.shape[0]
    local_heads = qkv_full.shape[2] // HD
    local_width = qkv_full.shape[2]
    local_hidden = up_full.shape[1]
    own_first = lax.axis_index("tensor") * own_rows
    positions = jnp.arange(group_rows, dtype=jnp.int32)
    seq_ids = positions // LEN
    length_rows = jnp.sum(
        jnp.where(
            seq_ids[:, None] == jnp.arange(seq_count, dtype=jnp.int32)[None, :], lengths[None, :], 0
        ),
        axis=1,
    )
    valid_all = (positions % LEN < length_rows).astype(jnp.float32)[:, None]
    valid_own = lax.dynamic_slice_in_dim(valid_all, own_first, own_rows, 0)
    own_count = jnp.sum(valid_own)
    tokens_in, cotangent_in = (
        lax.all_gather(tokens, "tensor", axis=0, tiled=True),
        lax.all_gather(cotangent, "tensor", axis=0, tiled=True),
    )

    def own_part(values):
        return lax.dynamic_slice_in_dim(values, own_first, own_rows, 0)

    def branch_total(source, weight):
        return lax.psum(
            jnp.dot(source, weight, preferred_element_type=jnp.float32).astype(jnp.bfloat16),
            "tensor",
        ).astype(jnp.float32)

    def input_total(source, weight):
        return lax.psum(contract_cols(source, weight).astype(jnp.bfloat16), "tensor").astype(
            jnp.float32
        )

    recorded = []

    def record(values):
        mine = own_part(values)
        square_sum = jnp.sum(valid_own * mine * mine)
        recorded.append(lax.psum((square_sum, own_count), ("dp", "tensor")))

    x_values = tokens_in.astype(jnp.float32)
    record(x_values)
    ln1_out, normed_one, spread_one = layer_norm(x_values, gain_one, shift_one)
    normed_a = ln1_out.astype(jnp.bfloat16)
    qkv_flat = qkv_full.reshape(D, 3 * local_width)
    projected = jnp.dot(normed_a, qkv_flat, preferred_element_type=jnp.float32)
    qv_values = qv_full.astype(jnp.float32)
    bias_all = jnp.stack([qv_values[0], jnp.zeros_like(qv_values[0]), qv_values[1]]).reshape(
        3 * local_width
    )
    qkv_low = (projected + bias_all).astype(jnp.bfloat16)
    qkv_seq = qkv_low.reshape(seq_count, LEN, 3, local_heads, HD)

    def forward_sequence(pair):
        seq_qkv, seq_len = pair
        return attend_forward(seq_qkv[:, 0], seq_qkv[:, 1], seq_qkv[:, 2], seq_len)

    attended, log_totals = lax.map(forward_sequence, (qkv_seq, lengths))
    attended_rows = attended.reshape(group_rows, local_width)
    attn_out = branch_total(attended_rows, out_full) + out_shift
    record(attn_out)
    middle = x_values + attn_out
    record(middle)
    ln2_out, normed_two, spread_two = layer_norm(middle, gain_two, shift_two)
    normed_c = ln2_out.astype(jnp.bfloat16)
    hidden_pre = jnp.dot(normed_c, up_full, preferred_element_type=jnp.float32) + up_shift.astype(
        jnp.float32
    ).reshape(local_hidden)
    hidden_act = gelu_tanh(hidden_pre).astype(jnp.bfloat16)
    mlp_out = branch_total(hidden_act, down_full) + down_shift
    record(mlp_out)
    result = middle + mlp_out
    record(result)
    grad_y = cotangent_in.astype(jnp.float32) * valid_all
    down_bias_grad = jnp.sum(own_part(grad_y), axis=0)
    grad_m = grad_y.astype(jnp.bfloat16)
    down_weight_grad = contract_rows(hidden_act, grad_m)
    grad_act = contract_cols(grad_m, down_full)
    gelu_value, gelu_back = jax.vjp(gelu_tanh, hidden_pre)
    grad_u = gelu_back(grad_act)[0].astype(jnp.bfloat16)
    up_bias_grad = jnp.sum(grad_u, axis=0, dtype=jnp.float32).reshape(local_hidden // 16, 16)
    up_weight_grad = contract_rows(normed_c, grad_u)
    grad_c = input_total(grad_u, up_full)
    grad_mid = grad_y + norm_backward(grad_c, normed_two, spread_two, gain_two)
    ln2_gain_grad = jnp.sum(own_part(grad_c * normed_two), axis=0)
    ln2_bias_grad = jnp.sum(own_part(grad_c), axis=0)
    out_bias_grad = jnp.sum(own_part(grad_mid), axis=0)
    grad_z = grad_mid.astype(jnp.bfloat16)
    out_weight_grad = contract_rows(attended_rows, grad_z)
    grad_o = contract_cols(grad_z, out_full).astype(jnp.bfloat16)
    grad_o_seq = grad_o.reshape(seq_count, LEN, local_heads, HD)

    def backward_sequence(group):
        seq_qkv, seq_grad, seq_totals, seq_len = group
        return attend_backward(
            seq_qkv[:, 0], seq_qkv[:, 1], seq_qkv[:, 2], seq_grad, seq_totals, seq_len
        )

    grad_q, grad_k, grad_v = lax.map(backward_sequence, (qkv_seq, grad_o_seq, log_totals, lengths))
    grad_qkv = jnp.stack([grad_q, grad_k, grad_v], axis=2).reshape(group_rows, 3 * local_width)
    qv_bias_grad = jnp.stack(
        [
            jnp.sum(grad_q, axis=(0, 1), dtype=jnp.float32),
            jnp.sum(grad_v, axis=(0, 1), dtype=jnp.float32),
        ]
    )
    qkv_weight_grad = contract_rows(normed_a, grad_qkv).reshape(D, 3, local_width)
    grad_a = input_total(grad_qkv, qkv_flat)
    grad_x_all = grad_mid + norm_backward(grad_a, normed_one, spread_one, gain_one)
    tokens_grad = own_part(grad_x_all)
    ln1_gain_grad = jnp.sum(own_part(grad_a * normed_one), axis=0)
    ln1_bias_grad = jnp.sum(own_part(grad_a), axis=0)
    (
        qkv_weight_out,
        qv_bias_out,
        out_weight_out,
        up_weight_out,
        up_bias_out,
        down_weight_out,
        ln1_gain_part,
        ln1_bias_part,
        out_bias_part,
        ln2_gain_part,
        ln2_bias_part,
        down_bias_part,
    ) = (
        lax.psum_scatter(
            qkv_weight_grad.astype(jnp.bfloat16), "dp", scatter_dimension=0, tiled=True
        ).astype(jnp.float32),
        lax.psum_scatter(
            qv_bias_grad.astype(jnp.bfloat16), "dp", scatter_dimension=2, tiled=True
        ).astype(jnp.float32),
        lax.psum_scatter(
            out_weight_grad.astype(jnp.bfloat16), "dp", scatter_dimension=1, tiled=True
        ).astype(jnp.float32),
        lax.psum_scatter(
            up_weight_grad.astype(jnp.bfloat16), "dp", scatter_dimension=0, tiled=True
        ).astype(jnp.float32),
        lax.psum_scatter(
            up_bias_grad.astype(jnp.bfloat16), "dp", scatter_dimension=1, tiled=True
        ).astype(jnp.float32),
        lax.psum_scatter(
            down_weight_grad.astype(jnp.bfloat16), "dp", scatter_dimension=1, tiled=True
        ).astype(jnp.float32),
        lax.psum_scatter(
            ln1_gain_grad.astype(jnp.bfloat16), "dp", scatter_dimension=0, tiled=True
        ).astype(jnp.float32),
        lax.psum_scatter(
            ln1_bias_grad.astype(jnp.bfloat16), "dp", scatter_dimension=0, tiled=True
        ).astype(jnp.float32),
        lax.psum_scatter(
            out_bias_grad.astype(jnp.bfloat16), "dp", scatter_dimension=0, tiled=True
        ).astype(jnp.float32),
        lax.psum_scatter(
            ln2_gain_grad.astype(jnp.bfloat16), "dp", scatter_dimension=0, tiled=True
        ).astype(jnp.float32),
        lax.psum_scatter(
            ln2_bias_grad.astype(jnp.bfloat16), "dp", scatter_dimension=0, tiled=True
        ).astype(jnp.float32),
        lax.psum_scatter(
            down_bias_grad.astype(jnp.bfloat16), "dp", scatter_dimension=0, tiled=True
        ).astype(jnp.float32),
    )
    ln1_gain_out, ln1_bias_out, out_bias_out, ln2_gain_out, ln2_bias_out, down_bias_out = lax.psum(
        (ln1_gain_part, ln1_bias_part, out_bias_part, ln2_gain_part, ln2_bias_part, down_bias_part),
        "tensor",
    )
    totals = jnp.stack([entry[0] for entry in recorded])
    count = recorded[0][1]
    stream_rms = jnp.sqrt(totals / (count * D))
    return (
        own_part(result).astype(jnp.bfloat16),
        tokens_grad,
        ln1_gain_out,
        ln1_bias_out,
        qkv_weight_out,
        qv_bias_out,
        out_weight_out,
        out_bias_out,
        ln2_gain_out,
        ln2_bias_out,
        up_weight_out,
        up_bias_out,
        down_weight_out,
        down_bias_out,
        stream_rms,
    )


def solution(mesh):
    placed = (
        P(("dp", "tensor"), None),
        P("dp"),
        P("dp"),
        P("dp"),
        P("dp", None, "tensor"),
        P(None, "tensor", "dp"),
        P("tensor", "dp"),
        P("dp"),
        P("dp"),
        P("dp"),
        P("dp", "tensor"),
        P("tensor", "dp"),
        P("tensor", "dp"),
        P("dp"),
        P(("dp", "tensor"), None),
    )
    return jax.shard_map(
        shards,
        mesh=mesh,
        in_specs=placed,
        out_specs=(
            P(("dp", "tensor"), None),
            P(("dp", "tensor"), None),
            P("dp"),
            P("dp"),
            P("dp", None, "tensor"),
            P(None, "tensor", "dp"),
            P("tensor", "dp"),
            P("dp"),
            P("dp"),
            P("dp"),
            P("dp", "tensor"),
            P("tensor", "dp"),
            P("tensor", "dp"),
            P("dp"),
            P(),
        ),
        check_vma=False,
    )
```

profile of v0, /device:TPU:0, one launch (start us, length us, event | category | flops | bytes accessed | tf_op | source)
XLA Modules:
  0.0 1390.4 jit_solution(11187329936646952826)
XLA Ops:
  12.4 10.4 all-gather.1
  22.8 8.9 all-gather
  32.5 8.3 all_gather.46
  41.2 51.9 %all-gather.14.cloned.1.call-done = bf16[1024,2048]{1,0:T(8,128)(2,1)} async-done(((bf16[256,2048]{1,0:T(8,128)(2,1)}), bf16[1024,2048]{1,0:T(8,128)(2,1)}) %all-gather.14.cloned.1.call-update) | async-done | bytes 4194320 | tf_op jit(solution)/shard_map/all_gather | solution.py:192
  93.1 2.8 convert_reduce_fusion
  95.9 3.4 multiply_reduce_fusion.4
  99.3 41.3 %all-gather.16.cloned.1.call-done = bf16[2048,3,512]{0,2,1:T(8,128)(2,1)} async-done(((bf16[256,3,512]{0,2,1:T(8,128)(2,1)}), bf16[2048,3,512]{0,2,1:T(8,128)(2,1)}) %all-gather.16.cloned.1.call-update) | async-done | bytes 6291472 | tf_op jit(solution)/shard_map/all_gather | solution.py:156
  140.6 12.5 add_convert_fusion.2
  153.1 6.3 squeeze.48
  159.4 3.1 fusion.85
  162.8 22.4 %while.50 = (s32[]{:T(128)}, bf16[2,512,4,128]{3,2,1,0:T(4,128)(2,1)}, f32[2,4,512]{2,1,0:T(4,128)S(1)}, s32[2]{0:T(128)S(1)}, s32[]{:T(128)}, /*index=5*/bf16[1...) while((s32[]{:T(128)}, ...), condition=%wide.region_5.6_spmd.clone.clone, body=%wide.region_2.5_spmd.clone.clone.sunk | while | flops 1100217856 | bytes 39917828 | solution.py:68
  169.3 3.1 fusion.130
  180.4 3.1 fusion.130
  185.3 7.0 convolution_convert_fusion.6
  195.1 8.8 all-gather.4
  203.9 8.1 all-gather.3
  212.0 8.8 all-gather.2
  220.8 8.0 all-gather.5
  229.0 118.4 %all-reduce.15.cloned.1.call-done = bf16[1024,2048]{1,0:T(8,128)(2,1)} async-done(((bf16[1024,2048]{1,0:T(8,128)(2,1)}), bf16[1024,2048]{1,0:T(8,128)(2,1)}) %all-reduce.15.cloned.1.call-update) | async-done | bytes 4194320 | tf_op jit(solution)/shard_map/psum | solution.py:200
  347.4 11.2 fusion.84
  358.6 4.5 multiply_reduce_fusion.3
  364.3 4.0 subtract_multiply_fusion
  368.3 34.0 %all-gather.20.cloned.1.call-done = bf16[2048,2048]{1,0:T(8,128)(2,1)} async-done(((bf16[256,2048]{1,0:T(8,128)(2,1)}), bf16[2048,2048]{1,0:T(8,128)(2,1)}) %all-gather.20.cloned.1.call-update) | async-done | bytes 8388624 | tf_op jit(solution)/shard_map/all_gather | solution.py:162
  402.4 15.9 %fusion.69 = f32[1024,2048]{1,0:T(8,128)} fusion(bf16[2048,2048]{1,0:T(8,128)(2,1)} %all-gather.20.cloned.1.call-done, f32[1024,2048]{1,0:T(8,128)} %subtract_multiply_fusion, f32[2048]{0:T(1024)S(1)} %bitcast.153, f32[2048]{0:T(1024)S(1)} %bitcast.140), kind=kOutput, calls=%fused_computation.120 | convolution fusion | flops 8596226048 | bytes 25182208 | tf_op jit(solution)/shard_map/dot_general | solution.py:242
  418.3 66.3 %all-gather.24.cloned.1.call-done = bf16[1024,2048]{1,0:T(8,128)(2,1)} async-done(((bf16[256,2048]{1,0:T(8,128)(2,1)}), bf16[1024,2048]{1,0:T(8,128)(2,1)}) %all-gather.24.cloned.1.call-update) | async-done | bytes 4194320 | tf_op jit(solution)/shard_map/all_gather | solution.py:193
  484.6 56.3 %all-gather.22.cloned.1.call-done = bf16[2048,2048]{1,0:T(8,128)(2,1)} async-done(((bf16[2048,256]{1,0:T(8,128)(2,1)}), bf16[2048,2048]{1,0:T(8,128)(2,1)}) %all-gather.22.cloned.1.call-update) | async-done | bytes 8388624 | tf_op jit(solution)/shard_map/all_gather | solution.py:164
  540.8 19.2 %fusion.87 = (bf16[2048]{0:T(1024)(128)(2,1)}, bf16[1024,2048]{1,0:T(8,128)(2,1)S(1)}) fusion(f32[1024,2048]{1,0:T(8,128)} %fusion.69, f32[2048]{0:T(1024)S(1)} %reshape.277, bf16[2048,2048]{1,0:T(8,128)(2,1)} %all-gather.22.cloned.1.call-done, f32[1024]{0:T(1024)S(1)} %fusion.82, bf16[1024,2048]{1,0:T(8,128)(2,1)} %all-gather.24.cloned.1.call-done), kind=kOutput, calls=%fused_computation.167 | convolution fusion | flops 8642361344 | bytes 25182208 | tf_op jit(solution)/shard_map/dot_general | solution.py:37
  562.1 13.1 convolution_convert_fusion.4
  575.3 155.1 %all-reduce.17.cloned.1.call-done = bf16[1024,2048]{1,0:T(8,128)(2,1)} async-done(((bf16[1024,2048]{1,0:T(8,128)(2,1)}), bf16[1024,2048]{1,0:T(8,128)(2,1)}) %all-reduce.17.cloned.1.call-update) | async-done | bytes 4194320 | tf_op jit(solution)/shard_map/psum | solution.py:206
  730.4 6.0 multiply_reduce_fusion.5
  737.5 8.4 convert_multiply_fusion
  745.8 6.5 fusion.66
  752.4 41.1 %while.51 = (s32[]{:T(128)}, f32[1024,4,128]{0,2,1:T(8,128)S(1)}, f32[1024,4,128]{0,2,1:T(8,128)}, bf16[2,512,4,128]{3,1,2,0:T(8,128)(2,1)}, s32[2]{0:T(128)S(1)...) while((s32[]{:T(128)}, f32[1024,4,128]{0,2,1:T(8,128)S(1)}, ...), condition=%wide.region_15.16_spmd.clone.clone, body=%wide.region_13.15_spmd.clone.clone.sunk | while | flops 2720005632 | bytes 100202928 | solution.py:113
  759.2 3.8 bitcast_add_fusion.5
  763.0 4.0 multiply_reduce_fusion.8
  767.1 2.4 multiply_convert_fusion.5
  779.1 5.1 bitcast_add_fusion.5
  784.2 4.0 multiply_reduce_fusion.8
  797.8 7.4 convolution_convert_fusion.7
  805.3 16.3 %convolution_convert_fusion.5 = bf16[1024,2048]{1,0:T(8,128)(2,1)} fusion(bf16[2048,2048]{1,0:T(8,128)(2,1)} %all-gather.22.cloned.1.call-done, f32[1024,2048]{1,0:T(8,128)} %fusion.69, f32[2048]{0:T(1024)S(1)} %copy-done.27), kind=kOutput, calls=%fused_computation.86 | convolution fusion | flops 8613003264 | bytes 20979712 | tf_op jit(solution)/shard_map/dot_general | solution.py:201
  824.1 3.5 pad_maximum_fusion
  827.6 4.7 copy.114
  832.3 11.2 convolution_convert_fusion.3
  844.2 20.2 %convolution_convert_fusion = bf16[2048,2048]{1,0:T(8,128)(2,1)} fusion(bf16[1024,2048]{1,0:T(8,128)(2,1)} %all-gather.24.cloned.1.call-done, f32[1024]{0:T(1024)S(1)} %copy-done.25, f32[1024,2048]{1,0:T(8,128)} %fusion.69, f32[2048]{0:T(1024)S(1)} %copy-done.27), kind=kOutput, calls=%fused_computation.77 | convolution fusion | flops 8621391872 | bytes 20983808 | tf_op jit(solution)/shard_map/dot_general | solution.py:31
  865.1 14.8 %convolution_convert_fusion.1 = bf16[2048,2048]{1,0:T(8,128)(2,1)} fusion(bf16[1024,2048]{1,0:T(8,128)(2,1)} %copy-done.39, f32[1024,2048]{1,0:T(8,128)} %subtract_multiply_fusion, f32[2048]{0:T(1024)S(1)} %bitcast.154, f32[2048]{0:T(1024)S(1)} %bitcast.143), kind=kOutput, calls=%fused_computation.78 | convolution fusion | flops 8600420352 | bytes 20987904 | tf_op jit(solution)/shard_map/dot_general | solution.py:31
  880.6 14.2 %convolution_convert_fusion.2 = bf16[2048,3,512]{2,0,1:T(8,128)(2,1)} fusion(bf16[3,512,1024]{2,1,0:T(8,128)(2,1)} %bitcast.135, f32[2048]{0:T(1024)S(1)} %bitcast.152, f32[2048]{0:T(1024)S(1)} %bitcast.145, bf16[1024,2048]{1,0:T(8,128)(2,1)} %all-gather.14.cloned.1.call-done, f32[1024]{0:T(1024)S(1)} %copy-done.23, f32[1024]{0:T(1024)S(1)} %copy-done.19), kind=kOutput, calls=%fused_computation.81 | convolution fusion | flops 6458179584 | bytes 13656064 | tf_op jit(solution)/shard_map/dot_general | solution.py:31
  896.7 9.1 all-gather.6
  906.6 6.5 convert_element_type.197
  913.2 3.3 convert_element_type.219
  923.4 243.2 %all-reduce.19.cloned.1.call-done = (bf16[1024,2048]{1,0:T(8,128)(2,1)}, bf16[1024,2048]{1,0:T(8,128)(2,1)}) async-done(((bf16[1024,2048]{1,0:T(8,128)(2,1)}, bf16[1024,2048]{1,0:T(8,128)(2,1)}), (bf16[1024,2048]{1,0:T(8,128)(2,1)}, bf16[1024,2048]{1,0:T(8,128)(2,1)})) %all-reduce.19.cloned.1.call-update) | async-done | bytes 8388624 | tf_op jit(solution)/shard_map/psum | solution.py:200
  1166.6 3.4 convert_add_fusion
  1170.0 5.6 fusion.52
  1175.6 40.5 %all-reduce.7 = (f32[1]{0:T(128)}, f32[1]{0:T(128)}, f32[1]{0:T(128)}, f32[1]{0:T(128)}, f32[1]{0:T(128)}, /*index=5*/f32[]{:T(128)}) all-reduce(f32[1]{0:T(128)} %bitcast.25, f32[1]{0:T(128)} %bitcast.26, f32[1]{0:T(128)} %bitcast.27, f32[1]{0:T(128)} %bitcast.28, ...), channel_id=1, replica_groups=mesh['dp'=8,'tensor'=4] {'dp','tensor'}, use_global_device_ids=true, to_apply=%region_47.48 | all-reduce | flops 6 | bytes 48 | tf_op jit(solution)/shard_map/psum | solution.py:215
  1216.1 6.7 convert_element_type.225
  1222.8 2.8 fusion.57
  1225.8 4.8 dynamic-slice_reduce_fusion.3
  1230.6 24.5 %all-reduce.9 = (bf16[2048]{0:T(1024)(128)(2,1)S(1)}, bf16[2048]{0:T(1024)(128)(2,1)S(1)}, bf16[2048]{0:T(1024)(128)(2,1)S(1)}, bf16[2048]{0:T(1024)(128)(2,1)S(...) all-reduce(bf16[2048]{0:T(1024)(128)(2,1)S(1)} %get-tuple-element.5, ...), channel_id=2, replica_groups=mesh['dp'=8,'tensor'=4] {'dp'}, use_global_device_ids=true, to_apply=%region_20.21.clone | all-reduce | flops 14336 | bytes 57344
  1256.6 3.4 stack.58
  1260.0 2.8 convert_element_type.248
  1262.7 53.5 %reduce-scatter.13.cloned.1.call-done = bf16[256,2048]{1,0:T(8,128)(2,1)} async-done(((bf16[2048,2048]{1,0:T(8,128)(2,1)}), bf16[256,2048]{1,0:T(8,128)(2,1)}) %reduce-scatter.13.cloned.1.call-update) | async-done | bytes 1048592 | tf_op jit(solution)/shard_map/reduce_scatter | solution.py:312
  1316.3 2.8 convert_element_type.244
  1319.5 12.5 all-reduce.8
  1332.5 48.7 %reduce-scatter.9.cloned.1.call-done = bf16[256,3,512]{2,0,1:T(8,128)(2,1)} async-done(((bf16[2048,3,512]{2,0,1:T(8,128)(2,1)}), bf16[256,3,512]{2,0,1:T(8,128)(2,1)}) %reduce-scatter.9.cloned.1.call-update) | async-done | bytes 786448 | tf_op jit(solution)/shard_map/reduce_scatter | solution.py:303
  1381.2 2.5 convert_element_type.231
  (228 shorter events, 63.1 us)
Async XLA Ops:
  7.2 85.9 %all-gather.14.cloned.1.call-start = ((), (), s32[]{:S(2)}) async-start(), calls=%async_computation.5 | async-start | bytes 5242880 | tf_op jit(solution)/shard_map/all_gather | solution.py:192
  7.9 132.7 %all-gather.16.cloned.1.call-start = ((), (), s32[]{:S(2)}) async-start(), calls=%async_computation.6 | async-start | bytes 7077888 | tf_op jit(solution)/shard_map/all_gather | solution.py:156
  10.3 175.0 %all-gather.18.cloned.1.call-start = ((), (), s32[]{:S(2)}) async-start(), calls=%async_computation.7 | async-start | bytes 2359296 | tf_op jit(solution)/shard_map/all_gather | solution.py:158
  11.0 336.4 %all-reduce.15.cloned.1.call-start = ((), (), s32[]{:S(2)}) async-start(), calls=%async_computation.8 | async-start | bytes 8388608 | tf_op jit(solution)/shard_map/psum | solution.py:200
  22.8 130.3 %copy-start.28 = (f32[8,1,256]{2,1,0:T(1,128)}, f32[8,1,256]{2,1,0:T(1,128)S(1)}, u32[]{:S(2)}) copy-start(f32[8,1,256]{2,1,0:T(1,128)S(1)} %convert_element_type.259) | copy-start | bytes 24580
  31.7 121.3 %copy-start.20 = (f32[8,1,256]{2,1,0:T(1,128)}, f32[8,1,256]{2,1,0:T(1,128)S(1)}, u32[]{:S(2)}) copy-start(f32[8,1,256]{2,1,0:T(1,128)S(1)} %convert_element_type.258) | copy-start | bytes 24580
  95.9 57.2 %copy-start.18 = (f32[1024]{0:T(1024)}, f32[1024]{0:T(1024)S(1)}, u32[]{:S(2)}) copy-start(f32[1024]{0:T(1024)S(1)} %broadcast_multiply_fusion.6) | copy-start | bytes 12292
  99.3 53.8 %copy-start.22 = (f32[1024]{0:T(1024)}, f32[1024]{0:T(1024)S(1)}, u32[]{:S(2)}) copy-start(f32[1024]{0:T(1024)S(1)} %add_rsqrt_fusion.1) | copy-start | bytes 12292
  169.3 3.2 copy-start.14
  173.0 1.0 copy-start.15
  180.4 3.2 copy-start.14
  184.1 1.0 copy-start.15
  185.2 7.7 copy-start.2
  185.2 7.7 copy-start.6
  185.3 9.7 copy-start.34
  185.3 9.7 copy-start.35
  185.3 9.7 copy-start.36
  185.3 35.5 %copy-start.33 = (bf16[128,2]{0,1:T(2,128)(2,1)S(1)}, bf16[128,2]{0,1:T(2,128)(2,1)}, u32[]{:S(2)}) copy-start(bf16[128,2]{0,1:T(2,128)(2,1)} %param.30) | copy-start | bytes 1540
  192.4 210.0 %all-gather.20.cloned.1.call-start = ((), (), s32[]{:S(2)}) async-start(), calls=%async_computation.9 | async-start | bytes 9437184 | tf_op jit(solution)/shard_map/all_gather | solution.py:162
  193.0 291.6 %all-gather.24.cloned.1.call-start = ((), (), s32[]{:S(2)}) async-start(), calls=%async_computation.11 | async-start | bytes 5242880 | tf_op jit(solution)/shard_map/all_gather | solution.py:193
  193.6 347.3 %all-gather.22.cloned.1.call-start = ((), (), s32[]{:S(2)}) async-start(), calls=%async_computation.10 | async-start | bytes 9437184 | tf_op jit(solution)/shard_map/all_gather | solution.py:164
  194.3 536.0 %all-reduce.17.cloned.1.call-start = ((), (), s32[]{:S(2)}) async-start(), calls=%async_computation.12 | async-start | bytes 8388608 | tf_op jit(solution)/shard_map/psum | solution.py:206
  203.9 198.5 %copy-start.30 = (f32[8,1,256]{2,1,0:T(1,128)}, f32[8,1,256]{2,1,0:T(1,128)S(1)}, u32[]{:S(2)}) copy-start(f32[8,1,256]{2,1,0:T(1,128)S(1)} %convert_element_type.262) | copy-start | bytes 24580
  212.0 524.4 %copy-start.16 = (f32[8,1,256]{2,1,0:T(1,128)}, f32[8,1,256]{2,1,0:T(1,128)S(1)}, u32[]{:S(2)}) copy-start(f32[8,1,256]{2,1,0:T(1,128)S(1)} %convert_element_type.261) | copy-start | bytes 24580
  228.9 311.9 %copy-start.26 = (f32[2048]{0:T(1024)}, f32[2048]{0:T(1024)S(1)}, u32[]{:S(2)}) copy-start(f32[2048]{0:T(1024)S(1)} %reshape.277) | copy-start | bytes 24580
  229.0 507.4 %copy-start.24 = (f32[1024]{0:T(1024)}, f32[1024]{0:T(1024)S(1)}, u32[]{:S(2)}) copy-start(f32[1024]{0:T(1024)S(1)} %fusion.82) | copy-start | bytes 12292
  358.6 5.8 copy-start
  560.0 2.1 copy-start.39
  575.2 344.9 %reduce-scatter.17.cloned.1.call-start = ((), (), s32[]{:S(2)}) async-start(), calls=%async_computation.17 | async-start | bytes 36864
  730.4 6.0 copy-start.5
  730.4 7.1 copy-start.10
  745.8 6.5 copy-start.4
  755.7 3.5 copy-start.9
  759.2 3.8 copy-start.7
  767.1 2.5 copy-start.11
  767.1 3.9 copy-start.3
  771.0 1.4 copy-start.12
  775.5 3.5 copy-start.9
  779.1 5.1 copy-start.7
  788.2 2.5 copy-start.11
  788.2 3.9 copy-start.3
  792.1 1.4 copy-start.12
  795.3 10.0 copy-start.27
  797.8 123.8 %reduce-scatter.11.cloned.1.call-start = ((), (), s32[]{:S(2)}) async-start(), calls=%async_computation.14 | async-start | bytes 2359296 | tf_op jit(solution)/shard_map/reduce_scatter | solution.py:309
  805.3 361.3 %all-reduce.19.cloned.1.call-start = ((), (), s32[]{:S(2)}) async-start(), calls=%async_computation.18 | async-start | bytes 16777216 | tf_op jit(solution)/shard_map/psum | solution.py:200
  805.3 16.4 %copy-start.13 = (bf16[2,512,4,128]{3,1,2,0:T(8,128)(2,1)S(1)}, bf16[2,512,4,128]{3,1,2,0:T(8,128)(2,1)}, u32[]{:S(2)}) copy-start(bf16[2,512,4,128]{3,1,2,0:T(8,128)(2,1)} %get-tuple-element.174) | copy-start | bytes 3145732
  843.5 0.7 copy-start.25
  843.5 416.4 %reduce-scatter.15.cloned.1.call-start = ((), (), s32[]{:S(2)}) async-start(), calls=%async_computation.16 | async-start | bytes 9437184 | tf_op jit(solution)/shard_map/reduce_scatter | solution.py:318
  864.4 0.7 copy-start.17
  864.4 0.7 copy-start.31
  864.4 451.8 %reduce-scatter.13.cloned.1.call-start = ((), (), s32[]{:S(2)}) async-start(), calls=%async_computation.15 | async-start | bytes 9437184 | tf_op jit(solution)/shard_map/reduce_scatter | solution.py:312
  879.9 0.7 copy-start.19
  879.9 0.7 copy-start.21
  879.9 0.7 copy-start.23
  879.9 0.7 copy-start.29
  880.0 501.2 %reduce-scatter.9.cloned.1.call-start = ((), (), s32[]{:S(2)}) async-start(), calls=%async_computation.13 | async-start | bytes 7077888 | tf_op jit(solution)/shard_map/reduce_scatter | solution.py:303
  880.6 14.2 %copy-start.38 = (u32[32]{0:T(128)S(1)}, u32[32]{0:T(128)}, u32[]{:S(2)}) copy-start(u32[32]{0:T(128)} %constant.157) | copy-start | bytes 388
  880.6 16.1 %copy-start.37 = (bf16[256]{0:T(256)(128)(2,1)S(1)}, bf16[256]{0:T(256)(128)(2,1)}, u32[]{:S(2)}) copy-start(bf16[256]{0:T(256)(128)(2,1)} %param.32) | copy-start | bytes 1540
  894.8 18.3 %copy-start.32 = (bf16[2048]{0:T(1024)(128)(2,1)S(1)}, bf16[2048]{0:T(1024)(128)(2,1)}, u32[]{:S(2)}) copy-start(bf16[2048]{0:T(1024)(128)(2,1)} %get-tuple-element.519) | copy-start | bytes 12292
  1216.1 6.7 copy-start.1
  1216.1 6.7 copy-start.8
Sparse Core Ops, SparseCore 0:
  9.6 83.4 all-gather.13
  95.5 45.0 all-gather.15
  142.5 28.0 all-gather.17
  192.5 154.8 all-reduce.14
  349.1 53.2 all-gather.19
  403.8 80.7 all-gather.23
  486.4 54.3 all-gather.21
  575.3 154.9 all-reduce.16
  797.9 30.3 reduce-scatter.16
  832.0 41.1 reduce-scatter.10
  875.7 290.8 all-reduce.18
  1169.9 71.3 reduce-scatter.14
  1244.7 71.4 reduce-scatter.12
  1319.5 61.6 reduce-scatter.8
where the time goes:
time: 1400 us; the launch traced here: 1390 us
  waiting for transfers between devices  872 us (62%)
  matrix products  195 us (14%)
  blocking collectives  148 us (11%)
  other arithmetic  108 us (8%)
  local copies, waits for them, and re-layouts  41.9 us (3%)
  between operations  17.3 us (1%)
    psum x2, waiting for transfers between devices, branch_total(): lax.psum(jnp.dot(source, weight, preferred_element_type=jnp.float32).asty...  362 us
    psum x1, waiting for transfers between devices, input_total(): lax.psum(contract_cols(source, weight).astype(jnp.bfloat16), 'tensor')  155 us
    all_gather x1, waiting for transfers between devices, shards(): lax.all_gather(cotangent, 'tensor', axis=0, tiled=True)  66.3 us
    dot_general x4, matrix products, contract_rows(): lax.dot_general(left, right, (((0,), (0,)), ((), ())), preferred_element_...  56.6 us
    all_gather x1, waiting for transfers between devices, shards(): lax.all_gather(down_weight, 'dp', axis=1, tiled=True)  56.3 us
    reduce_scatter x1, waiting for transfers between devices, shards(): lax.psum_scatter(up_weight_grad.astype(jnp.bfloat16), 'dp', scatter_dimen...  53.5 us
    all_gather x1, waiting for transfers between devices, shards(): lax.all_gather(tokens, 'tensor', axis=0, tiled=True)  51.9 us
    dot_general x4, matrix products, contract_cols(): lax.dot_general(left, right, (((1,), (1,)), ((), ())), preferred_element_...  50 us
  transfers between devices with their start and end apart: 14, of which 10 were waited for; matrix products, arithmetic and copies ran while one was open for 17% of the time, Pallas kernels for 0%

commit v1 on v0

--- a/solution.py
+++ b/solution.py
@@ -7,6 +7,10 @@
 HD = 128
 LEN = 1024
 EPS = 1e-05
+
+
+def measure_point(here_x):
+    return lax.all_gather(here_x, "tensor").sum(axis=0)
 
 
 def layer_norm(values, norm_gain, norm_shift):
@@ -197,9 +201,8 @@
         return lax.dynamic_slice_in_dim(values, own_first, own_rows, 0)
 
     def branch_total(source, weight):
-        return lax.psum(
-            jnp.dot(source, weight, preferred_element_type=jnp.float32).astype(jnp.bfloat16),
-            "tensor",
+        return measure_point(
+            jnp.dot(source, weight, preferred_element_type=jnp.float32).astype(jnp.bfloat16)
         ).astype(jnp.float32)
 
     def input_total(source, weight):

time: 1400 us -> 1760 us (1.26)
  waiting for transfers between devices: 872 us -> 1200 us
  other arithmetic: 108 us -> 130 us
    all_gather x0 -> x2, waiting for transfers between devices: none -> 536 us  [measure_point(): return lax.all_gather(here_x, 'tensor').sum(axis=0)]
    psum x2 -> x0, waiting for transfers between devices: 362 us -> none  [branch_total(): lax.psum(jnp.dot(source, weight, preferred_element_type=jnp.float32).asty...]
    psum x1 -> x2, waiting for transfers between devices: 155 us -> 265 us  [input_total(): lax.psum(contract_cols(source, weight).astype(jnp.bfloat16), 'tensor')]
    reduce_scatter x1, waiting for transfers between devices: 0.01 us -> 72 us  [shards(): lax.psum_scatter(down_weight_grad.astype(jnp.bfloat16), 'dp', scatter_dim...]
    reduce_scatter x1, waiting for transfers between devices: 53.5 us -> 26.8 us  [shards(): lax.psum_scatter(up_weight_grad.astype(jnp.bfloat16), 'dp', scatter_dimen...]
    reduce_sum x0 -> x2, other arithmetic: none -> 24.3 us  [measure_point(): return lax.all_gather(here_x, 'tensor').sum(axis=0)]
  transfers between devices with their start and end apart: 14 -> 15, of which waited for: 10 -> 12; matrix products, arithmetic and copies ran while one was open for 17% -> 13% of each run, Pallas kernels for 0% -> 0%
where the time goes in v1:
time: 1760 us
  waiting for transfers between devices  1200 us (68%)
  matrix products  212 us (12%)
  blocking collectives  144 us (8%)
  other arithmetic  130 us (7%)
  local copies, waits for them, and re-layouts  42.3 us (2%)
  between operations  17.6 us (1%)
    all_gather x2, waiting for transfers between devices, measure_point(): return lax.all_gather(here_x, 'tensor').sum(axis=0)  536 us
    psum x2, waiting for transfers between devices, input_total(): lax.psum(contract_cols(source, weight).astype(jnp.bfloat16), 'tensor')  265 us
    reduce_scatter x1, waiting for transfers between devices, shards(): lax.psum_scatter(down_weight_grad.astype(jnp.bfloat16), 'dp', scatter_dim...  72 us
    all_gather x1, waiting for transfers between devices, shards(): lax.all_gather(cotangent, 'tensor', axis=0, tiled=True)  66.6 us
    reduce_scatter x1, waiting for transfers between devices, shards(): lax.psum_scatter(qkv_weight_grad.astype(jnp.bfloat16), 'dp', scatter_dime...  62.2 us
    all_gather x1, waiting for transfers between devices, shards(): lax.all_gather(down_weight, 'dp', axis=1, tiled=True)  56.3 us
    dot_general x4, matrix products, contract_rows(): lax.dot_general(left, right, (((0,), (0,)), ((), ())), preferred_element_...  55.2 us
    all_gather x1, waiting for transfers between devices, shards(): lax.all_gather(tokens, 'tensor', axis=0, tiled=True)  51.9 us
  transfers between devices with their start and end apart: 15, of which 12 were waited for; matrix products, arithmetic and copies ran while one was open for 13% of the time, Pallas kernels for 0%

profile of v1, /device:TPU:0, one launch (start us, length us, event | category | flops | bytes accessed | tf_op | source)
XLA Modules:
  0.0 1755.9 jit_solution(9753565067106414055)
XLA Ops:
  11.9 10.7 all_gather.58
  23.7 8.9 all-gather.2
  33.2 7.9 all-gather.3
  41.2 51.9 %all-gather.18.cloned.1.call-done = bf16[1024,2048]{1,0:T(8,128)(2,1)} async-done(((bf16[256,2048]{1,0:T(8,128)(2,1)}), bf16[1024,2048]{1,0:T(8,128)(2,1)}) %all-gather.18.cloned.1.call-update) | async-done | bytes 4194320 | tf_op jit(solution)/shard_map/all_gather | solution.py:196
  95.9 3.4 multiply_reduce_fusion.4
  99.3 41.3 %all-gather.20.cloned.1.call-done = bf16[2048,3,512]{0,2,1:T(8,128)(2,1)} async-done(((bf16[256,3,512]{0,2,1:T(8,128)(2,1)}), bf16[2048,3,512]{0,2,1:T(8,128)(2,1)}) %all-gather.20.cloned.1.call-update) | async-done | bytes 6291472 | tf_op jit(solution)/shard_map/all_gather | solution.py:160
  140.6 12.6 add_convert_fusion.2
  153.2 5.0 squeeze.48
  159.7 22.2 %while.50 = (s32[]{:T(128)}, bf16[2,512,4,128]{3,2,1,0:T(4,128)(2,1)}, f32[2,4,512]{2,1,0:T(4,128)S(1)}, s32[2]{0:T(128)S(1)}, s32[]{:T(128)}, /*index=5*/bf16[1...) while((s32[]{:T(128)}, ...), condition=%wide.region_5.6_spmd.clone.clone, body=%wide.region_2.5_spmd.clone.clone.sunk | while | flops 1100217856 | bytes 31529664 | solution.py:72
  177.1 3.1 fusion.130
  182.0 6.9 convolution_convert_fusion.6
  191.5 8.9 all-gather.4
  200.4 8.0 all-gather.5
  208.5 8.9 all-gather.6
  217.4 7.9 all-gather.7
  225.5 250.3 %all-gather.30.cloned.1.call-done = bf16[4096,2048]{1,0:T(8,128)(2,1)} async-done(((bf16[1024,2048]{1,0:T(8,128)(2,1)}), bf16[4096,2048]{1,0:T(8,128)(2,1)}) %all-gather.30.cloned.1.call-update) | async-done | bytes 16777232 | tf_op jit(solution)/shard_map/all_gather | solution.py:13
  475.8 12.3 reduce_sum.258
  488.1 10.6 fusion.84
  498.7 4.5 multiply_reduce_fusion.3
  505.2 4.0 subtract_multiply_fusion
  509.2 20.8 %all-gather.24.cloned.1.call-done = bf16[2048,2048]{1,0:T(8,128)(2,1)} async-done(((bf16[256,2048]{1,0:T(8,128)(2,1)}), bf16[2048,2048]{1,0:T(8,128)(2,1)}) %all-gather.24.cloned.1.call-update) | async-done | bytes 8388624 | tf_op jit(solution)/shard_map/all_gather | solution.py:166
  530.0 15.6 fusion.69
  545.6 66.6 %all-gather.28.cloned.1.call-done = bf16[1024,2048]{1,0:T(8,128)(2,1)} async-done(((bf16[256,2048]{1,0:T(8,128)(2,1)}), bf16[1024,2048]{1,0:T(8,128)(2,1)}) %all-gather.28.cloned.1.call-update) | async-done | bytes 4194320 | tf_op jit(solution)/shard_map/all_gather | solution.py:197
  612.2 56.3 %all-gather.26.cloned.1.call-done = bf16[2048,2048]{1,0:T(8,128)(2,1)} async-done(((bf16[2048,256]{1,0:T(8,128)(2,1)}), bf16[2048,2048]{1,0:T(8,128)(2,1)}) %all-gather.26.cloned.1.call-update) | async-done | bytes 8388624 | tf_op jit(solution)/shard_map/all_gather | solution.py:168
  668.4 19.3 %fusion.87 = (bf16[2048]{0:T(1024)(128)(2,1)}, bf16[1024,2048]{1,0:T(8,128)(2,1)S(1)}) fusion(f32[1024,2048]{1,0:T(8,128)} %fusion.69, f32[2048]{0:T(1024)S(1)} %reshape.277, bf16[2048,2048]{1,0:T(8,128)(2,1)} %all-gather.26.cloned.1.call-done, f32[1024]{0:T(1024)S(1)} %fusion.82, bf16[1024,2048]{1,0:T(8,128)(2,1)} %all-gather.28.cloned.1.call-done), kind=kOutput, calls=%fused_computation.167 | convolution fusion | flops 8642361344 | bytes 25182208 | tf_op jit(solution)/shard_map/dot_general | solution.py:41
  689.7 12.6 convolution_convert_fusion.4
  702.5 155.1 %all-reduce.13.cloned.1.call-done = bf16[1024,2048]{1,0:T(8,128)(2,1)} async-done(((bf16[1024,2048]{1,0:T(8,128)(2,1)}), bf16[1024,2048]{1,0:T(8,128)(2,1)}) %all-reduce.13.cloned.1.call-update) | async-done | bytes 4194320 | tf_op jit(solution)/shard_map/psum | solution.py:209
  857.5 6.0 multiply_reduce_fusion.5
  864.6 8.3 convert_multiply_fusion
  872.9 6.5 fusion.66
  879.4 66.1 %while.51 = (s32[]{:T(128)}, f32[1024,4,128]{0,2,1:T(8,128)S(1)}, f32[1024,4,128]{0,2,1:T(8,128)}, bf16[2,512,4,128]{3,1,2,0:T(8,128)(2,1)}, s32[2]{0:T(128)S(1)...) while((s32[]{:T(128)}, f32[1024,4,128]{0,2,1:T(8,128)S(1)}, ...), condition=%wide.region_15.16_spmd.clone.clone, body=%wide.region_13.15_spmd.clone.clone.sunk | while | flops 2720005632 | bytes 171506224 | solution.py:117
  881.1 5.5 fusion.140
  889.6 7.7 multiply_reduce_fusion.8
  897.4 3.7 multiply_convert_fusion.5
  901.1 3.8 bitcast_add_fusion.4
  908.2 3.8 bitcast_add_fusion.5
  913.3 5.5 fusion.140
  921.9 7.7 multiply_reduce_fusion.8
  929.6 3.7 multiply_convert_fusion.5
  933.4 3.8 bitcast_add_fusion.4
  940.5 5.0 bitcast_add_fusion.5
  950.2 7.4 convolution_convert_fusion.7
  966.4 11.3 convolution_convert_fusion.3
  977.8 14.6 convolution_convert_fusion.1
  993.1 20.2 %convolution_convert_fusion = bf16[2048,2048]{1,0:T(8,128)(2,1)} fusion(bf16[1024,2048]{1,0:T(8,128)(2,1)} %all-gather.28.cloned.1.call-done, f32[1024]{0:T(1024)S(1)} %copy-done.23, f32[1024,2048]{1,0:T(8,128)} %fusion.69, f32[2048]{0:T(1024)S(1)} %copy-done.25), kind=kOutput, calls=%fused_computation.77 | convolution fusion | flops 8621391872 | bytes 20983808 | tf_op jit(solution)/shard_map/dot_general | solution.py:35
  1015.2 13.1 convolution_convert_fusion.2
  1028.6 16.2 convolution_convert_fusion.5
  1044.9 8.7 all-gather.8
  1056.3 6.5 convert_element_type.201
  1062.9 3.3 convert_element_type.223
  1073.1 109.6 %all-reduce.15.cloned.1.call-done = bf16[1024,2048]{1,0:T(8,128)(2,1)} async-done(((bf16[1024,2048]{1,0:T(8,128)(2,1)}), bf16[1024,2048]{1,0:T(8,128)(2,1)}) %all-reduce.15.cloned.1.call-update) | async-done | bytes 4194320 | tf_op jit(solution)/shard_map/psum | solution.py:209
  1182.7 5.3 fusion.57
  1189.3 4.4 dynamic-slice_reduce_fusion.3
  1193.6 24.4 %all-reduce.9 = (bf16[2048]{0:T(1024)(128)(2,1)S(1)}, bf16[2048]{0:T(1024)(128)(2,1)S(1)}, bf16[2048]{0:T(1024)(128)(2,1)S(1)}, bf16[2048]{0:T(1024)(128)(2,1)S(...) all-reduce(bf16[2048]{0:T(1024)(128)(2,1)S(1)} %get-tuple-element.5, ...), channel_id=4, replica_groups=mesh['dp'=8,'tensor'=4] {'dp'}, use_global_device_ids=true, to_apply=%region_20.21.clone | all-reduce | flops 14336 | bytes 57344
  1219.2 10.7 all-reduce.8
  1229.9 26.8 %reduce-scatter.13.cloned.1.call-done = bf16[256,2048]{1,0:T(8,128)(2,1)} async-done(((bf16[2048,2048]{1,0:T(8,128)(2,1)}), bf16[256,2048]{1,0:T(8,128)(2,1)}) %reduce-scatter.13.cloned.1.call-update) | async-done | bytes 1048592 | tf_op jit(solution)/shard_map/reduce_scatter | solution.py:315
  1259.5 72.0 %reduce-scatter.15.cloned.1.call-done = bf16[2048,256]{1,0:T(8,128)(2,1)} async-done(((bf16[2048,2048]{1,0:T(8,128)(2,1)}), bf16[2048,256]{1,0:T(8,128)(2,1)}) %reduce-scatter.15.cloned.1.call-update) | async-done | bytes 1048592 | tf_op jit(solution)/shard_map/reduce_scatter | solution.py:321
  1334.2 62.2 %reduce-scatter.9.cloned.1.call-done = bf16[256,3,512]{2,0,1:T(8,128)(2,1)} async-done(((bf16[2048,3,512]{2,0,1:T(8,128)(2,1)}), bf16[256,3,512]{2,0,1:T(8,128)(2,1)}) %reduce-scatter.9.cloned.1.call-update) | async-done | bytes 786448 | tf_op jit(solution)/shard_map/reduce_scatter | solution.py:306
  1398.9 285.7 %all-gather.32.cloned.1.call-done = bf16[4096,2048]{1,0:T(8,128)(2,1)} async-done(((bf16[1024,2048]{1,0:T(8,128)(2,1)}), bf16[4096,2048]{1,0:T(8,128)(2,1)}) %all-gather.32.cloned.1.call-update) | async-done | bytes 16777232 | tf_op jit(solution)/shard_map/all_gather | solution.py:13
  1684.6 12.0 reduce_sum.261
  1696.6 3.4 convert_add_fusion
  1700.0 5.7 fusion.52
  1705.7 38.8 %all-reduce.7 = (f32[1]{0:T(128)}, f32[1]{0:T(128)}, f32[1]{0:T(128)}, f32[1]{0:T(128)}, f32[1]{0:T(128)}, /*index=5*/f32[]{:T(128)}) all-reduce(f32[1]{0:T(128)} %bitcast.27, f32[1]{0:T(128)} %bitcast.28, f32[1]{0:T(128)} %bitcast.29, f32[1]{0:T(128)} %bitcast.30, ...), channel_id=1, replica_groups=mesh['dp'=8,'tensor'=4] {'dp','tensor'}, use_global_device_ids=true, to_apply=%region_47.48 | all-reduce | flops 6 | bytes 48 | tf_op jit(solution)/shard_map/psum | solution.py:218
  1745.2 3.2 stack.58
  (239 shorter events, 80.9 us)
Async XLA Ops:
  7.2 85.9 %all-gather.18.cloned.1.call-start = ((), (), s32[]{:S(2)}) async-start(), calls=%async_computation.5 | async-start | bytes 5242880 | tf_op jit(solution)/shard_map/all_gather | solution.py:196
  7.9 132.7 %all-gather.20.cloned.1.call-start = ((), (), s32[]{:S(2)}) async-start(), calls=%async_computation.6 | async-start | bytes 7077888 | tf_op jit(solution)/shard_map/all_gather | solution.py:160
  10.3 171.6 %all-gather.22.cloned.1.call-start = ((), (), s32[]{:S(2)}) async-start(), calls=%async_computation.7 | async-start | bytes 2359296 | tf_op jit(solution)/shard_map/all_gather | solution.py:162
  11.0 464.8 %all-gather.30.cloned.1.call-start = ((), (), s32[]{:S(2)}) async-start(), calls=%async_computation.17 | async-start | bytes 20971520 | tf_op jit(solution)/shard_map/all_gather | solution.py:13
  32.6 108.1 %copy-start.18 = (f32[8,1,256]{2,1,0:T(1,128)}, f32[8,1,256]{2,1,0:T(1,128)S(1)}, u32[]{:S(2)}) copy-start(f32[8,1,256]{2,1,0:T(1,128)S(1)} %convert_element_type.262) | copy-start | bytes 24580
  41.2 99.4 %copy-start.26 = (f32[8,1,256]{2,1,0:T(1,128)}, f32[8,1,256]{2,1,0:T(1,128)S(1)}, u32[]{:S(2)}) copy-start(f32[8,1,256]{2,1,0:T(1,128)S(1)} %convert_element_type.263) | copy-start | bytes 24580
  95.9 44.7 %copy-start.16 = (f32[1024]{0:T(1024)}, f32[1024]{0:T(1024)S(1)}, u32[]{:S(2)}) copy-start(f32[1024]{0:T(1024)S(1)} %broadcast_multiply_fusion.6) | copy-start | bytes 12292
  99.3 41.3 %copy-start.20 = (f32[1024]{0:T(1024)}, f32[1024]{0:T(1024)S(1)}, u32[]{:S(2)}) copy-start(f32[1024]{0:T(1024)S(1)} %add_rsqrt_fusion.1) | copy-start | bytes 12292
  181.9 7.6 copy-start.5
  181.9 7.6 copy-start.8
  181.9 9.6 copy-start.32
  181.9 18.5 %copy-start.33 = (bf16[256]{0:T(256)(128)(2,1)S(1)}, bf16[256]{0:T(256)(128)(2,1)}, u32[]{:S(2)}) copy-start(bf16[256]{0:T(256)(128)(2,1)} %param.27) | copy-start | bytes 1540
  181.9 26.5 %copy-start.34 = (bf16[256]{0:T(256)(128)(2,1)S(1)}, bf16[256]{0:T(256)(128)(2,1)}, u32[]{:S(2)}) copy-start(bf16[256]{0:T(256)(128)(2,1)} %param.28) | copy-start | bytes 1540
  181.9 35.4 %copy-start.31 = (bf16[128,2]{0,1:T(2,128)(2,1)S(1)}, bf16[128,2]{0,1:T(2,128)(2,1)}, u32[]{:S(2)}) copy-start(bf16[128,2]{0,1:T(2,128)(2,1)} %param.30) | copy-start | bytes 1540
  188.9 341.1 %all-gather.24.cloned.1.call-start = ((), (), s32[]{:S(2)}) async-start(), calls=%async_computation.8 | async-start | bytes 9437184 | tf_op jit(solution)/shard_map/all_gather | solution.py:166
  189.5 422.7 %all-gather.28.cloned.1.call-start = ((), (), s32[]{:S(2)}) async-start(), calls=%async_computation.10 | async-start | bytes 5242880 | tf_op jit(solution)/shard_map/all_gather | solution.py:197
  190.1 478.4 %all-gather.26.cloned.1.call-start = ((), (), s32[]{:S(2)}) async-start(), calls=%async_computation.9 | async-start | bytes 9437184 | tf_op jit(solution)/shard_map/all_gather | solution.py:168
  190.8 666.7 %all-reduce.13.cloned.1.call-start = ((), (), s32[]{:S(2)}) async-start(), calls=%async_computation.11 | async-start | bytes 8388608 | tf_op jit(solution)/shard_map/psum | solution.py:209
  217.4 312.6 %copy-start.28 = (f32[8,1,256]{2,1,0:T(1,128)}, f32[8,1,256]{2,1,0:T(1,128)S(1)}, u32[]{:S(2)}) copy-start(f32[8,1,256]{2,1,0:T(1,128)S(1)} %convert_element_type.266) | copy-start | bytes 24580
  225.4 443.0 %copy-start.24 = (f32[2048]{0:T(1024)}, f32[2048]{0:T(1024)S(1)}, u32[]{:S(2)}) copy-start(f32[2048]{0:T(1024)S(1)} %reshape.277) | copy-start | bytes 24580
  225.4 638.1 %copy-start.22 = (f32[1024]{0:T(1024)}, f32[1024]{0:T(1024)S(1)}, u32[]{:S(2)}) copy-start(f32[1024]{0:T(1024)S(1)} %fusion.82) | copy-start | bytes 12292
  498.7 6.5 copy-start.2
  687.8 2.0 copy-start.37
  702.4 367.5 %reduce-scatter.17.cloned.1.call-start = ((), (), s32[]{:S(2)}) async-start(), calls=%async_computation.19 | async-start | bytes 36864
  857.5 6.0 copy-start.7
  857.5 7.1 copy-start.12
  872.9 6.5 copy-start.6
  889.2 8.2 slice-start
  889.6 7.7 copy-start.3
  889.6 7.7 slice-start.1
  901.1 3.8 copy-start.1
  901.1 3.9 copy-start.13
  901.1 6.5 copy-start
  901.1 6.8 copy-start.4
  901.1 7.1 copy-start.11
  906.4 1.0 copy-start.14
  921.4 8.2 slice-start
  921.9 7.7 copy-start.3
  921.9 7.7 slice-start.1
  933.3 3.8 copy-start.1
  933.3 3.9 copy-start.13
  933.3 6.5 copy-start
  933.4 6.8 copy-start.4
  933.4 7.1 copy-start.11
  938.6 1.0 copy-start.14
  947.3 12.7 copy-start.10
  950.0 121.3 %reduce-scatter.11.cloned.1.call-start = ((), (), s32[]{:S(2)}) async-start(), calls=%async_computation.14 | async-start | bytes 2359296 | tf_op jit(solution)/shard_map/reduce_scatter | solution.py:312
  957.7 225.1 %all-reduce.15.cloned.1.call-start = ((), (), s32[]{:S(2)}) async-start(), calls=%async_computation.12 | async-start | bytes 8388608 | tf_op jit(solution)/shard_map/psum | solution.py:209
  966.4 11.4 copy-start.29
  977.7 279.0 %reduce-scatter.13.cloned.1.call-start = ((), (), s32[]{:S(2)}) async-start(), calls=%async_computation.15 | async-start | bytes 9437184 | tf_op jit(solution)/shard_map/reduce_scatter | solution.py:315
  992.4 0.7 copy-start.23
  992.4 0.7 copy-start.25
  992.4 339.1 %reduce-scatter.15.cloned.1.call-start = ((), (), s32[]{:S(2)}) async-start(), calls=%async_computation.16 | async-start | bytes 9437184 | tf_op jit(solution)/shard_map/reduce_scatter | solution.py:321
  1013.3 1.9 copy-start.15
  1013.3 1.9 copy-start.17
  1013.3 1.9 copy-start.19
  1013.3 1.9 copy-start.21
  1013.3 1.9 copy-start.27
  1013.3 383.1 %reduce-scatter.9.cloned.1.call-start = ((), (), s32[]{:S(2)}) async-start(), calls=%async_computation.13 | async-start | bytes 7077888 | tf_op jit(solution)/shard_map/reduce_scatter | solution.py:306
  1028.3 16.6 copy-start.35
  1028.3 25.3 %copy-start.36 = (u32[32]{0:T(128)S(1)}, u32[32]{0:T(128)}, u32[]{:S(2)}) copy-start(u32[32]{0:T(128)} %constant.159) | copy-start | bytes 388
  1028.3 656.3 %all-gather.32.cloned.1.call-start = ((), (), s32[]{:S(2)}) async-start(), calls=%async_computation.18 | async-start | bytes 20971520 | tf_op jit(solution)/shard_map/all_gather | solution.py:13
  1044.8 17.9 %copy-start.30 = (bf16[2048]{0:T(1024)(128)(2,1)S(1)}, bf16[2048]{0:T(1024)(128)(2,1)}, u32[]{:S(2)}) copy-start(bf16[2048]{0:T(1024)(128)(2,1)} %get-tuple-element.517) | copy-start | bytes 12292
  1182.7 5.5 copy-start.9
Sparse Core Ops, SparseCore 0:
  9.6 83.4 all-gather.17
  95.5 45.0 all-gather.19
  142.5 28.0 all-gather.21
  189.0 286.7 all-gather.29
  477.5 52.4 all-gather.23
  531.4 80.7 all-gather.27
  614.1 54.3 all-gather.25
  702.5 154.9 all-reduce.12
  950.1 30.2 reduce-scatter.16
  984.2 41.1 reduce-scatter.10
  1027.7 154.9 all-reduce.14
  1186.0 70.6 reduce-scatter.12
  1260.2 71.2 reduce-scatter.14
  1334.7 61.6 reduce-scatter.8
  1397.8 286.7 all-gather.31
